TPU v7x, 32 devices: a whole 2x2x4 slice. The times are simulated.
32 devices in a mesh: row: 8 (over z, x), col: 4 (over y, core).
Axes of the slice: x: 2, y: 2, z: 4, core: 2. Of those that a mesh axis runs over, the one named last changes fastest.
Arguments:
- receptance: bfloat16 [2, 16384, 16384], P(None, 'row', 'col'), may hold values from -4 to 60, as said below
- coupling: int32 [2, 768], replicated, may hold values from 0 to 16383, as said below
Outputs:
- coupled: bfloat16 [2, 16384, 16384], P(None, 'row', 'col')
Inputs may be any that keep to these rules, and one draw needn't show every extreme that they name: `coupling`: row 0 holds 768 distinct body DOFs, all in the first half of the 16384 DOFs; row 1 holds 768 distinct cavity DOFs, all in the second half. `receptance`: the driving-point entry of every body or cavity DOF named in coupling (same response and excitation DOF) has real part 52 or more; every other real or imaginary part lies within -4 to 4.
All inputs are finite; a program needn't handle non-finite values.
Results may differ from a plain program's by a relative error of at most 0.015.
Values may be sent and summed in bfloat16 or wider, within the bound.
A program may use at most 320 MiB of HBM per device.

v0:
```python
import jax
import jax.numpy as jnp
from jax import lax
from jax.sharding import PartitionSpec as P

SWEEPS = 6


def select_rows(matrix, body_dof, cav_dof, offset, extent):
    count = body_dof.shape[0]
    both_dof = jnp.concatenate([body_dof, cav_dof]) - offset
    inside = (both_dof >= 0) & (both_dof < extent)
    clipped = jnp.clip(both_dof, 0, extent - 1)
    picked = jnp.take(matrix, clipped, axis=1).astype(jnp.float32)
    picked = jnp.where(inside[None, :, None], picked, jnp.zeros((), jnp.float32))
    return picked[:, :count, :] - picked[:, count:, :]


def select_columns(matrix, body_dof, cav_dof, offset, extent):
    positions = offset + lax.broadcasted_iota(jnp.int32, (extent, 1), 0)
    table = (positions == body_dof[None, :]).astype(jnp.float32) - (
        positions == cav_dof[None, :]
    ).astype(jnp.float32)
    table = table.astype(matrix.dtype)
    return jnp.einsum(
        "prc,cn->prn",
        matrix,
        table,
        preferred_element_type=jnp.float32,
        precision=lax.Precision.HIGHEST,
    )


def complex_times(mat_real, mat_imag, vec_real, vec_imag):
    hi = lax.Precision.HIGHEST
    out_real = jnp.dot(mat_real, vec_real, precision=hi) - jnp.dot(mat_imag, vec_imag, precision=hi)
    out_imag = jnp.dot(mat_real, vec_imag, precision=hi) + jnp.dot(mat_imag, vec_real, precision=hi)
    return (out_real, out_imag)


def local(receptance, coupling):
    tile_rows = receptance.shape[1]
    tile_cols = receptance.shape[2]
    row_index = lax.axis_index("row")
    col_index = lax.axis_index("col")
    body_dof = coupling[0]
    cav_dof = coupling[1]
    row_terms = select_rows(receptance, body_dof, cav_dof, row_index * tile_rows, tile_rows)
    rhs_local = lax.psum_scatter(
        row_terms.astype(jnp.bfloat16), "row", scatter_dimension=2, tiled=True
    ).astype(jnp.float32)
    solve_cols = rhs_local.shape[2]
    column_terms = select_columns(receptance, body_dof, cav_dof, col_index * tile_cols, tile_cols)
    left_full = lax.psum(column_terms.astype(jnp.bfloat16), "col")
    first_col = col_index * tile_cols + row_index * solve_cols
    inter_terms = select_columns(rhs_local, body_dof, cav_dof, first_col, solve_cols)
    interface = lax.psum(inter_terms, ("row", "col"))
    z_real = interface[0]
    z_imag = interface[1]
    diag_real = jnp.diagonal(z_real)
    diag_imag = jnp.diagonal(z_imag)
    modulus = diag_real * diag_real + diag_imag * diag_imag
    d_real = (diag_real / modulus)[:, None]
    d_imag = (-diag_imag / modulus)[:, None]

    def scale(part_real, part_imag):
        return (d_real * part_real - d_imag * part_imag, d_real * part_imag + d_imag * part_real)

    v_real = rhs_local[0]
    v_imag = rhs_local[1]
    x_real, x_imag = scale(v_real, v_imag)
    for sweep_index in range(SWEEPS):
        p_real, p_imag = complex_times(z_real, z_imag, x_real, x_imag)
        e_real, e_imag = scale(v_real - p_real, v_imag - p_imag)
        x_real = x_real + e_real
        x_imag = x_imag + e_imag
    weights = jnp.stack([x_real, x_imag]).astype(jnp.bfloat16)
    u_real = left_full[0]
    u_imag = left_full[1]
    column_piece = lax.all_gather(weights, "row", axis=2, tiled=True)
    p_real = column_piece[0]
    p_imag = column_piece[1]
    c_real = jnp.dot(u_real, p_real, preferred_element_type=jnp.float32) - jnp.dot(
        u_imag, p_imag, preferred_element_type=jnp.float32
    )
    c_imag = jnp.dot(u_real, p_imag, preferred_element_type=jnp.float32) + jnp.dot(
        u_imag, p_real, preferred_element_type=jnp.float32
    )
    recv_piece = receptance.astype(jnp.float32)
    return (recv_piece - jnp.stack([c_real, c_imag])).astype(jnp.bfloat16)


def solution(mesh):
    in_specs = (P(None, "row", "col"), P())
    out_specs = P(None, "row", "col")
    return jax.shard_map(local, mesh=mesh, in_specs=in_specs, out_specs=out_specs, check_vma=False)
```

profile of v0, /device:TPU:0, one launch (start us, length us, event | category | flops | bytes accessed | tf_op | source)
XLA Modules:
  0.0 973.6 jit_solution(2592334917314808475)
XLA Ops:
  7.4 93.4 %gather_fusion = bf16[1536,2,4096]{2,0,1:T(8,128)(2,1)} fusion(bf16[2,2048,4096]{2,1,0:T(8,128)(2,1)} %param.2, s32[2048]{0:T(1024)S(1)} %pad_clamp_fusion), kind=kCustom, calls=%fused_computation | custom fusion | bytes 50337792 | tf_op jit(solution)/shard_map/jit(_take)/gather | solution.py:14
  100.8 27.7 %select_bitcast_fusion = f32[2,1536,4096]{2,1,0:T(8,128)} fusion(bf16[1536,2,4096]{2,0,1:T(8,128)(2,1)} %gather_fusion, pred[1536]{0:T(1024)(128)(4,1)S(1)} %get-tuple-element.24, pred[1536]{0:T(1024)(128)(4,1)S(1)} %get-tuple-element.23), kind=kLoop, calls=%fused_computation.5 | loop fusion | flops 37748736 | bytes 75500544 | tf_op jit(solution)/shard_map/jit(_where)/select_n | solution.py:15
  128.5 21.2 %fusion.1 = bf16[2,768,4096]{2,1,0:T(8,128)(2,1)} fusion(f32[2,1536,4096]{2,1,0:T(8,128)} %select_bitcast_fusion), kind=kLoop, calls=%fused_computation.9 | loop fusion | flops 12582912 | bytes 62914560 | tf_op jit(solution)/shard_map/convert_element_type | solution.py:50
  149.8 207.7 %reduce-scatter.2.cloned.1.call-done = bf16[2,768,512]{2,1,0:T(8,128)(2,1)} async-done(((bf16[2,768,4096]{2,1,0:T(8,128)(2,1)}), bf16[2,768,512]{2,1,0:T(8,128)(2,1)}) %reduce-scatter.2.cloned.1.call-update) | async-done | bytes 1572880 | tf_op jit(solution)/shard_map/reduce_scatter | solution.py:49
  357.5 7.8 fusion.24
  365.4 31.4 %convert_bitcast_fusion = bf16[2,2048,768]{1,2,0:T(8,128)(2,1)} fusion(bf16[2,2048,4096]{2,1,0:T(8,128)(2,1)} %param.2, s32[4096]{0:T(1024)S(1)} %iota_add_fusion, s32[768]{0:T(1024)S(1)} %get-tuple-element.6, s32[768]{0:T(1024)S(1)} %get-tuple-element.5), kind=kOutput, calls=%fused_computation.15 | convolution fusion | flops 25791823872 | bytes 39868416 | tf_op jit(solution)/shard_map/prc,cn->prn/dot_general | solution.py:25
  400.3 108.9 %all-reduce.5.cloned.1.call-done = f32[2,768,768]{2,1,0:T(8,128)} async-done(((f32[2,768,768]{2,1,0:T(8,128)}), f32[2,768,768]{2,1,0:T(8,128)}) %all-reduce.5.cloned.1.call-update) | async-done | bytes 4718608 | tf_op jit(solution)/shard_map/psum | solution.py:57
  513.4 12.4 %gather_fusion.1 = f32[768]{0:T(1024)S(1)} fusion(f32[768,768]{1,0:T(8,128)} %get-tuple-element.9, s32[768]{0:T(1024)S(1)} %or_reduce_fusion), kind=kCustom, calls=%fused_computation.1 | custom fusion | bytes 12288 | tf_op jit(solution)/shard_map/jit(diagonal)/cond/branch_0_fun/gather | solution.py:60
  525.8 6.5 gather_fusion.2
  532.3 6.9 fusion.12
  539.2 6.9 fusion.14
  550.3 5.1 fusion.21
  567.2 4.8 subtract_add_fusion.3
  583.7 4.5 subtract_add_fusion.2
  600.2 4.3 subtract_add_fusion.1
  612.3 4.4 bitcast_subtract_fusion.7
  616.7 4.3 subtract_add_fusion
  633.0 4.5 fusion.35
  638.8 175.8 %all-gather.2.cloned.1.call-done = bf16[2,768,4096]{2,1,0:T(8,128)(2,1)} async-done(((bf16[2,768,512]{2,1,0:T(8,128)(2,1)}), bf16[2,768,4096]{2,1,0:T(8,128)(2,1)}) %all-gather.2.cloned.1.call-update) | async-done | bytes 12582928 | tf_op jit(solution)/shard_map/all_gather | solution.py:80
  814.6 23.2 %fusion.9 = f32[2048,4096]{1,0:T(8,128)} fusion(bf16[2,768,4096]{2,1,0:T(8,128)(2,1)} %all-gather.2.cloned.1.call-done, bf16[2,2048,768]{1,2,0:T(8,128)(2,1)} %all-reduce.3.cloned.1.call-done), kind=kOutput, calls=%fused_computation.20 | convolution fusion | flops 12884901888 | bytes 42991616 | tf_op jit(solution)/shard_map/dot_general | solution.py:86
  837.8 20.2 %fusion.8 = f32[2048,4096]{1,0:T(8,128)} fusion(bf16[2,768,4096]{2,1,0:T(8,128)(2,1)} %all-gather.2.cloned.1.call-done, bf16[2,2048,768]{1,2,0:T(8,128)(2,1)S(1)} %copy-done.2), kind=kOutput, calls=%fused_computation.19 | convolution fusion | flops 12884901888 | bytes 42991616 | tf_op jit(solution)/shard_map/dot_general | solution.py:83
  858.1 33.0 %add_bitcast_fusion = f32[1,2048,4096]{2,1,0:T(8,128)} fusion(f32[2048,4096]{1,0:T(8,128)} %fusion.9, bf16[2,768,4096]{2,1,0:T(8,128)(2,1)} %all-gather.2.cloned.1.call-done, bf16[2,2048,768]{1,2,0:T(8,128)(2,1)} %all-reduce.3.cloned.1.call-done), kind=kOutput, calls=%fused_computation.6 | convolution fusion | flops 12893290496 | bytes 76546048 | tf_op jit(solution)/shard_map/dot_general | solution.py:86
  891.0 33.3 %subtract_bitcast_fusion = f32[1,2048,4096]{2,1,0:T(8,128)} fusion(f32[2048,4096]{1,0:T(8,128)} %fusion.8, bf16[2,768,4096]{2,1,0:T(8,128)(2,1)} %all-gather.2.cloned.1.call-done, bf16[2,2048,768]{1,2,0:T(8,128)(2,1)} %all-reduce.3.cloned.1.call-done), kind=kOutput, calls=%fused_computation.7 | convolution fusion | flops 12893290496 | bytes 76546048 | tf_op jit(solution)/shard_map/dot_general | solution.py:83
  924.3 42.3 %fusion = bf16[2,2048,4096]{2,1,0:T(8,128)(2,1)} fusion(f32[1,2048,4096]{2,1,0:T(8,128)} %add_bitcast_fusion, f32[1,2048,4096]{2,1,0:T(8,128)} %subtract_bitcast_fusion, bf16[2,2048,4096]{2,1,0:T(8,128)(2,1)} %param.2), kind=kLoop, calls=%fused_computation.4 | loop fusion | flops 67108864 | bytes 134217728 | tf_op jit(solution)/shard_map/convert_element_type | solution.py:90
  (46 shorter events, 69.2 us)
Async XLA Ops:
  6.5 351.0 %reduce-scatter.2.cloned.1.call-start = ((), (), s32[]{:S(2)}) async-start(), calls=%async_computation.2 | async-start | bytes 14155776 | tf_op jit(solution)/shard_map/reduce_scatter | solution.py:49
  149.7 359.5 %all-reduce.5.cloned.1.call-start = ((), (), s32[]{:S(2)}) async-start(), calls=%async_computation.3 | async-start | bytes 9437184 | tf_op jit(solution)/shard_map/psum | solution.py:57
  365.4 273.4 %all-reduce.3.cloned.1.call-start = ((), (), s32[]{:S(2)}) async-start(), calls=%async_computation.1 | async-start | bytes 12582912 | tf_op jit(solution)/shard_map/psum | solution.py:54
  396.8 1.4 copy-start.1
  396.8 417.8 %all-gather.2.cloned.1.call-start = ((), (), s32[]{:S(2)}) async-start(), calls=%async_computation.4 | async-start | bytes 14155776 | tf_op jit(solution)/shard_map/all_gather | solution.py:80
  525.7 20.3 %slice-start = ((s8[4718592]{0:T(1024)(128)(4,1)}), s8[524288]{0:T(1024)(128)(4,1)S(1)}, s32[]{:S(2)}) async-start(s8[4718592]{0:T(1024)(128)(4,1)} %bitcast.150), calls=%async_computation.5 | async-start | bytes 1048576
  532.3 13.8 %slice-start.1 = ((s8[4718592]{0:T(1024)(128)(4,1)}), s8[4194304]{0:T(1024)(128)(4,1)S(1)}, s32[]{:S(2)}) async-start(s8[4718592]{0:T(1024)(128)(4,1)} %bitcast.150), calls=%async_computation.6 | async-start | bytes 8388608
  539.2 6.9 copy-start
  814.6 23.2 %copy-start.2 = (bf16[2,2048,768]{1,2,0:T(8,128)(2,1)S(1)}, bf16[2,2048,768]{1,2,0:T(8,128)(2,1)}, u32[]{:S(2)}) copy-start(bf16[2,2048,768]{1,2,0:T(8,128)(2,1)} %all-reduce.3.cloned.1.call-done) | copy-start | bytes 18874372
Sparse Core Ops, SparseCore 0:
  149.8 207.6 reduce-scatter.1
  365.5 143.7 all-reduce.4
  511.8 118.4 all-reduce.2
  638.9 175.7 all-gather.1
where the time goes:
time: 984 us; the launch traced here: 974 us
  waiting for transfers between devices  493 us (50%)
  matrix products  254 us (26%)
  local copies, waits for them, and re-layouts  119 us (12%)
  other arithmetic  94.7 us (10%)
  between operations  13.9 us (1%)
    reduce_scatter x1, waiting for transfers between devices, local(): lax.psum_scatter(row_terms.astype(jnp.bfloat16), 'row', scatter_dimension...  208 us
    all_gather x1, waiting for transfers between devices, local(): column_piece = lax.all_gather(weights, 'row', axis=2, tiled=True)  176 us
    psum x1, waiting for transfers between devices, local(): interface = lax.psum(inter_terms, ('row', 'col'))  109 us
    gather x1, local copies, waits for them, and re-layouts, select_rows(): picked = jnp.take(matrix, clipped, axis=1).astype(jnp.float32)  93.4 us
    convert_element_type x1, other arithmetic, local(): return (recv_piece - jnp.stack([c_real, c_imag])).astype(jnp.bfloat16)  42.3 us
    dot_general x2, matrix products, select_columns(): jnp.einsum('prc,cn->prn', matrix, table, preferred_element_type=jnp.float...  39.2 us
    dot_general x1, matrix products, local(): jnp.dot(u_imag, p_imag, preferred_element_type=jnp.float32)  33.3 us
    dot_general x1, matrix products, local(): jnp.dot(u_imag, p_real, preferred_element_type=jnp.float32)  33 us
  transfers between devices with their start and end apart: 4, of which 3 were waited for; matrix products, arithmetic and copies ran while one was open for 17% of the time, Pallas kernels for 0%

commit v1 on v0

--- a/solution.py
+++ b/solution.py
@@ -4,6 +4,12 @@
 from jax.sharding import PartitionSpec as P
 
 SWEEPS = 6
+
+
+def in_order(pieces, dim):
+    shape = list(pieces.shape[1:])
+    shape[dim] *= pieces.shape[0]
+    return jnp.moveaxis(pieces, 0, dim).reshape(shape)
 
 
 def select_rows(matrix, body_dof, cav_dof, offset, extent):
@@ -77,7 +83,19 @@
     weights = jnp.stack([x_real, x_imag]).astype(jnp.bfloat16)
     u_real = left_full[0]
     u_imag = left_full[1]
-    column_piece = lax.all_gather(weights, "row", axis=2, tiled=True)
+    peers = lax.axis_size("row")
+    pairs = [(i, (i + 1) % peers) for i in range(peers)]
+    back = [(b, a) for a, b in pairs]
+    lower, upper = ([], [])
+    for step in range(peers - 1):
+        if step % 2 == 0:
+            lower.append(lax.ppermute(lower[-1] if lower else weights, "row", pairs))
+        else:
+            upper.append(lax.ppermute(upper[-1] if upper else weights, "row", back))
+    blocks = jnp.stack([*lower[::-1], weights, *upper])
+    shift = lax.axis_index("row") - len(lower)
+    blocks = blocks[(jnp.arange(peers) - shift) % peers]
+    column_piece = in_order(blocks, 2)
     p_real = column_piece[0]
     p_imag = column_piece[1]
     c_real = jnp.dot(u_real, p_real, preferred_element_type=jnp.float32) - jnp.dot(

time: 984 us -> 1140 us (1.16)
  local copies, waits for them, and re-layouts: 119 us -> 175 us
  waiting for transfers between devices: 493 us -> 539 us
  starting transfers between devices: 0.13 us -> 45.7 us
    all_gather x1 -> x0, waiting for transfers between devices: 176 us -> none  [local(): column_piece = lax.all_gather(weights, 'row', axis=2, tiled=True)]
    ppermute x0 -> x7, waiting for transfers between devices: none -> 164 us  [the longest x4 164 us: local(): lower.append(lax.ppermute(lower[-1] if lower else weights, 'row', pairs))]
    ppermute x0 -> x7, starting transfers between devices: none -> 45.6 us  [the longest x3 39.2 us: local(): upper.append(lax.ppermute(upper[-1] if upper else weights, 'row', back))]
    psum x1, waiting for transfers between devices: 109 us -> 141 us  [local(): interface = lax.psum(inter_terms, ('row', 'col'))]
    slice x0 -> x3, local copies, waits for them, and re-layouts: none -> 28.2 us  [the longest x2 19.5 us: local(): p_real = column_piece[0]]
    psum x1, waiting for transfers between devices: 0.02 us -> 27.2 us  [local(): left_full = lax.psum(column_terms.astype(jnp.bfloat16), 'col')]
    unnamed x10 -> x22, local copies, waits for them, and re-layouts: 1.35 us -> 17.8 us
  transfers between devices with their start and end apart: 4 -> 10, of which waited for: 3 -> 7; matrix products, arithmetic and copies ran while one was open for 17% -> 8% of each run, Pallas kernels for 0% -> 0%
where the time goes in v1:
time: 1140 us; the launch traced here: 1130 us
  waiting for transfers between devices  539 us (47%)
  matrix products  256 us (22%)
  local copies, waits for them, and re-layouts  175 us (15%)
  other arithmetic  94.8 us (8%)
  starting transfers between devices  45.7 us (4%)
  between operations  15.6 us (1%)
    reduce_scatter x1, waiting for transfers between devices, local(): lax.psum_scatter(row_terms.astype(jnp.bfloat16), 'row', scatter_dimension...  208 us
    ppermute x4, waiting for transfers between devices, local(): lower.append(lax.ppermute(lower[-1] if lower else weights, 'row', pairs))  164 us
    psum x1, waiting for transfers between devices, local(): interface = lax.psum(inter_terms, ('row', 'col'))  141 us
    gather x1, local copies, waits for them, and re-layouts, select_rows(): picked = jnp.take(matrix, clipped, axis=1).astype(jnp.float32)  93.4 us
    convert_element_type x1, other arithmetic, local(): return (recv_piece - jnp.stack([c_real, c_imag])).astype(jnp.bfloat16)  42.3 us
    dot_general x2, matrix products, select_columns(): jnp.einsum('prc,cn->prn', matrix, table, preferred_element_type=jnp.float...  39.3 us
    ppermute x3, starting transfers between devices, local(): upper.append(lax.ppermute(upper[-1] if upper else weights, 'row', back))  39.2 us
    dot_general x1, matrix products, local(): jnp.dot(u_imag, p_imag, preferred_element_type=jnp.float32)  33.3 us
  transfers between devices with their start and end apart: 10, of which 7 were waited for; matrix products, arithmetic and copies ran while one was open for 8% of the time, Pallas kernels for 0%

profile of v1, /device:TPU:0, one launch (start us, length us, event | category | flops | bytes accessed | tf_op | source)
XLA Modules:
  0.0 1126.4 jit_solution(15829516180710175419)
XLA Ops:
  8.2 93.4 %gather_fusion = bf16[1536,2,4096]{2,0,1:T(8,128)(2,1)} fusion(bf16[2,2048,4096]{2,1,0:T(8,128)(2,1)} %param.2, s32[2048]{0:T(1024)S(1)} %pad_clamp_fusion), kind=kCustom, calls=%fused_computation | custom fusion | bytes 50337792 | tf_op jit(solution)/shard_map/jit(_take)/gather | solution.py:20
  101.7 27.7 %select_bitcast_fusion = f32[2,1536,4096]{2,1,0:T(8,128)} fusion(bf16[1536,2,4096]{2,0,1:T(8,128)(2,1)} %gather_fusion, pred[1536]{0:T(1024)(128)(4,1)S(1)} %get-tuple-element.26, pred[1536]{0:T(1024)(128)(4,1)S(1)} %get-tuple-element.25), kind=kLoop, calls=%fused_computation.6 | loop fusion | flops 37748736 | bytes 75500544 | tf_op jit(solution)/shard_map/jit(_where)/select_n | solution.py:21
  129.4 21.2 %fusion.1 = bf16[2,768,4096]{2,1,0:T(8,128)(2,1)} fusion(f32[2,1536,4096]{2,1,0:T(8,128)} %select_bitcast_fusion), kind=kLoop, calls=%fused_computation.10 | loop fusion | flops 12582912 | bytes 62914560 | tf_op jit(solution)/shard_map/convert_element_type | solution.py:56
  150.6 207.7 %reduce-scatter.2.cloned.1.call-done = bf16[2,768,512]{2,1,0:T(8,128)(2,1)} async-done(((bf16[2,768,4096]{2,1,0:T(8,128)(2,1)}), bf16[2,768,512]{2,1,0:T(8,128)(2,1)}) %reduce-scatter.2.cloned.1.call-update) | async-done | bytes 1572880 | tf_op jit(solution)/shard_map/reduce_scatter | solution.py:55
  358.4 7.8 fusion.24
  369.7 140.5 %all-reduce.5.cloned.1.call-done = f32[2,768,768]{2,1,0:T(8,128)} async-done(((f32[2,768,768]{2,1,0:T(8,128)}), f32[2,768,768]{2,1,0:T(8,128)}) %all-reduce.5.cloned.1.call-update) | async-done | bytes 4718608 | tf_op jit(solution)/shard_map/psum | solution.py:63
  514.3 12.4 %gather_fusion.1 = f32[768]{0:T(1024)S(1)} fusion(f32[768,768]{1,0:T(8,128)} %get-tuple-element.11, s32[768]{0:T(1024)S(1)} %or_reduce_fusion), kind=kCustom, calls=%fused_computation.1 | custom fusion | bytes 12288 | tf_op jit(solution)/shard_map/jit(diagonal)/cond/branch_0_fun/gather | solution.py:66
  533.1 6.9 fusion.12
  639.7 36.1 %collective-permute-done = bf16[2,768,512]{2,1,0:T(8,128)(2,1)S(1)} collective-permute-done((bf16[2,768,512]{2,1,0:T(8,128)(2,1)S(1)}, bf16[2,768,512]{2,1,0:T(8,128)(2,1)S(1)}, u32[]{:S(2)}, u32[]{:S(2)}) %collective-permute-start) | collective-permute-done | bytes 1572896 | tf_op jit(solution)/shard_map/ppermute | solution.py:92
  681.7 60.5 %collective-permute-done.1 = bf16[2,768,512]{2,1,0:T(8,128)(2,1)S(1)} collective-permute-done((bf16[2,768,512]{2,1,0:T(8,128)(2,1)S(1)}, bf16[2,768,512]{2,1,0:T(8,128)(2,1)S(1)}, u32[]{:S(2)}, u32[]{:S(2)}) %collective-permute-start.1) | collective-permute-done | bytes 1572896 | tf_op jit(solution)/shard_map/ppermute | solution.py:92
  745.9 32.3 %collective-permute-start.5 = (bf16[2,768,512]{2,1,0:T(8,128)(2,1)}, bf16[2,768,512]{2,1,0:T(8,128)(2,1)}, u32[]{:S(2)}, u32[]{:S(2)}) collective-permute-start(bf16[2,768,512]{2,1,0:T(8,128)(2,1)} %collective-permute-done.4), channel_id=1, source_target_pairs={{4,0},{8,4},{12,8},{16,12},{20,16},{24,20},{28,24},{0,28},{5,1},{9... | collective-permute-start | bytes 4718600 | tf_op jit(solution)/shard_map/ppermute | solution.py:94
  778.2 34.2 %collective-permute-done.2 = bf16[2,768,512]{2,1,0:T(8,128)(2,1)} collective-permute-done((bf16[2,768,512]{2,1,0:T(8,128)(2,1)S(1)}, bf16[2,768,512]{2,1,0:T(8,128)(2,1)}, u32[]{:S(2)}, u32[]{:S(2)}) %collective-permute-start.2) | collective-permute-done | bytes 1572896 | tf_op jit(solution)/shard_map/ppermute | solution.py:92
  815.0 31.4 %convert_bitcast_fusion = bf16[2,2048,768]{1,2,0:T(8,128)(2,1)} fusion(bf16[2,2048,4096]{2,1,0:T(8,128)(2,1)} %param.2, s32[4096]{0:T(1024)S(1)} %iota_add_fusion, s32[768]{0:T(1024)S(1)} %get-tuple-element.6, s32[768]{0:T(1024)S(1)} %get-tuple-element.5), kind=kOutput, calls=%fused_computation.14 | convolution fusion | flops 25791823872 | bytes 39868416 | tf_op jit(solution)/shard_map/prc,cn->prn/dot_general | solution.py:31
  848.7 32.9 %collective-permute-done.3 = bf16[2,768,512]{2,1,0:T(8,128)(2,1)} collective-permute-done((bf16[2,768,512]{2,1,0:T(8,128)(2,1)}, bf16[2,768,512]{2,1,0:T(8,128)(2,1)}, u32[]{:S(2)}, u32[]{:S(2)}) %collective-permute-start.3) | collective-permute-done | bytes 1572896 | tf_op jit(solution)/shard_map/ppermute | solution.py:92
  898.2 11.3 %gather_fusion.3 = bf16[8,2,768,512]{3,2,1,0:T(8,128)(2,1)} fusion(bf16[8,2,768,512]{3,2,1,0:T(8,128)(2,1)} %bitcast_dynamic-update-slice_fusion, s32[1024]{0:T(1024)S(1)} %pad_clamp_fusion.1), kind=kCustom, calls=%fused_computation.3 | custom fusion | bytes 25165856 | tf_op jit(solution)/shard_map/gather | solution.py:97
  909.4 11.0 fusion.59
  920.4 8.5 copy.3
  929.0 8.7 copy.4
  937.6 27.2 %all-reduce.3.cloned.1.call-done = bf16[2,2048,768]{1,2,0:T(8,128)(2,1)} async-done(((bf16[2,2048,768]{1,2,0:T(8,128)(2,1)}), bf16[2,2048,768]{1,2,0:T(8,128)(2,1)}) %all-reduce.3.cloned.1.call-update) | async-done | bytes 6291472 | tf_op jit(solution)/shard_map/psum | solution.py:60
  964.8 22.6 %fusion.10 = f32[2048,4096]{1,0:T(8,128)} fusion(bf16[768,4096]{0,1:T(8,128)(2,1)} %bitcast.170, bf16[2,2048,768]{1,2,0:T(8,128)(2,1)} %all-reduce.3.cloned.1.call-done), kind=kOutput, calls=%fused_computation.20 | convolution fusion | flops 12884901888 | bytes 42991616 | tf_op jit(solution)/shard_map/dot_general | solution.py:104
  987.4 22.4 %fusion.11 = f32[2048,4096]{1,0:T(8,128)} fusion(bf16[768,4096]{0,1:T(8,128)(2,1)} %bitcast.172, bf16[2,2048,768]{1,2,0:T(8,128)(2,1)} %all-reduce.3.cloned.1.call-done), kind=kOutput, calls=%fused_computation.21 | convolution fusion | flops 12884901888 | bytes 42991616 | tf_op jit(solution)/shard_map/dot_general | solution.py:101
  1009.9 33.1 %add_bitcast_fusion = f32[1,2048,4096]{2,1,0:T(8,128)} fusion(f32[2048,4096]{1,0:T(8,128)} %fusion.10, bf16[768,4096]{0,1:T(8,128)(2,1)} %bitcast.173, bf16[2,2048,768]{1,2,0:T(8,128)(2,1)} %all-reduce.3.cloned.1.call-done), kind=kOutput, calls=%fused_computation.7 | convolution fusion | flops 12893290496 | bytes 76546048 | tf_op jit(solution)/shard_map/dot_general | solution.py:104
  1042.9 33.3 %subtract_bitcast_fusion = f32[1,2048,4096]{2,1,0:T(8,128)} fusion(f32[2048,4096]{1,0:T(8,128)} %fusion.11, bf16[768,4096]{0,1:T(8,128)(2,1)} %bitcast.171, bf16[2,2048,768]{1,2,0:T(8,128)(2,1)} %all-reduce.3.cloned.1.call-done), kind=kOutput, calls=%fused_computation.8 | convolution fusion | flops 12893290496 | bytes 76546048 | tf_op jit(solution)/shard_map/dot_general | solution.py:101
  1076.2 42.3 %fusion = bf16[2,2048,4096]{2,1,0:T(8,128)(2,1)} fusion(f32[1,2048,4096]{2,1,0:T(8,128)} %add_bitcast_fusion, f32[1,2048,4096]{2,1,0:T(8,128)} %subtract_bitcast_fusion, bf16[2,2048,4096]{2,1,0:T(8,128)(2,1)} %param.2), kind=kLoop, calls=%fused_computation.5 | loop fusion | flops 67108864 | bytes 134217728 | tf_op jit(solution)/shard_map/convert_element_type | solution.py:108
  (77 shorter events, 145.3 us)
Async XLA Ops:
  7.4 351.0 %reduce-scatter.2.cloned.1.call-start = ((), (), s32[]{:S(2)}) async-start(), calls=%async_computation.2 | async-start | bytes 14155776 | tf_op jit(solution)/shard_map/reduce_scatter | solution.py:55
  150.6 359.6 %all-reduce.5.cloned.1.call-start = ((), (), s32[]{:S(2)}) async-start(), calls=%async_computation.3 | async-start | bytes 9437184 | tf_op jit(solution)/shard_map/psum | solution.py:63
  366.2 1.4 copy-start.5
  366.2 598.6 %all-reduce.3.cloned.1.call-start = ((), (), s32[]{:S(2)}) async-start(), calls=%async_computation.1 | async-start | bytes 12582912 | tf_op jit(solution)/shard_map/psum | solution.py:60
  526.7 20.1 %slice-start = ((s8[4718592]{0:T(1024)(128)(4,1)}), s8[524288]{0:T(1024)(128)(4,1)S(1)}, s32[]{:S(2)}) async-start(s8[4718592]{0:T(1024)(128)(4,1)} %bitcast.163), calls=%async_computation.4 | async-start | bytes 1048576
  533.1 13.8 %slice-start.1 = ((s8[4718592]{0:T(1024)(128)(4,1)}), s8[4194304]{0:T(1024)(128)(4,1)S(1)}, s32[]{:S(2)}) async-start(s8[4718592]{0:T(1024)(128)(4,1)} %bitcast.163), calls=%async_computation.5 | async-start | bytes 8388608
  540.0 6.9 copy-start
  638.4 37.4 %collective-permute-start = (bf16[2,768,512]{2,1,0:T(8,128)(2,1)S(1)}, bf16[2,768,512]{2,1,0:T(8,128)(2,1)S(1)}, u32[]{:S(2)}, u32[]{:S(2)}) collective-permute-start(bf16[2,768,512]{2,1,0:T(8,128)(2,1)S(1)} %pad_maximum_fusion), channel_id=1, source_target_pairs={{0,4},{4,8},{8,12},{12,16},{16,20},{20,24},{24,28},{28,0},{1,5},{5... | collective-permute-start | bytes 4718600 | tf_op jit(solution)/shard_map/ppermute | solution.py:92
  675.8 1.2 copy-start.1
  677.0 65.2 %collective-permute-start.1 = (bf16[2,768,512]{2,1,0:T(8,128)(2,1)S(1)}, bf16[2,768,512]{2,1,0:T(8,128)(2,1)S(1)}, u32[]{:S(2)}, u32[]{:S(2)}) collective-permute-start(bf16[2,768,512]{2,1,0:T(8,128)(2,1)S(1)} %collective-permute-done), channel_id=1, source_target_pairs={{0,4},{4,8},{8,12},{12,16},{16,20},{20,24},{24,28},{28,0},{1,5},{5... | collective-permute-start | bytes 4718600 | tf_op jit(solution)/shard_map/ppermute | solution.py:92
  677.0 68.9 %collective-permute-start.4 = (bf16[2,768,512]{2,1,0:T(8,128)(2,1)S(1)}, bf16[2,768,512]{2,1,0:T(8,128)(2,1)}, u32[]{:S(2)}, u32[]{:S(2)}) collective-permute-start(bf16[2,768,512]{2,1,0:T(8,128)(2,1)S(1)} %pad_maximum_fusion), channel_id=1, source_target_pairs={{4,0},{8,4},{12,8},{16,12},{20,16},{24,20},{28,24},{0,28},{5,1},{9... | collective-permute-start | bytes 4718600 | tf_op jit(solution)/shard_map/ppermute | solution.py:94
  742.2 1.2 copy-start.3
  743.4 69.0 %collective-permute-start.2 = (bf16[2,768,512]{2,1,0:T(8,128)(2,1)S(1)}, bf16[2,768,512]{2,1,0:T(8,128)(2,1)}, u32[]{:S(2)}, u32[]{:S(2)}) collective-permute-start(bf16[2,768,512]{2,1,0:T(8,128)(2,1)S(1)} %collective-permute-done.1), channel_id=1, source_target_pairs={{0,4},{4,8},{8,12},{12,16},{16,20},{20,24},{24,28},{28,0},{1,5},{5... | collective-permute-start | bytes 4718600 | tf_op jit(solution)/shard_map/ppermute | solution.py:92
  745.9 100.6 %collective-permute-start.5 = (bf16[2,768,512]{2,1,0:T(8,128)(2,1)}, bf16[2,768,512]{2,1,0:T(8,128)(2,1)}, u32[]{:S(2)}, u32[]{:S(2)}) collective-permute-start(bf16[2,768,512]{2,1,0:T(8,128)(2,1)} %collective-permute-done.4), channel_id=1, source_target_pairs={{4,0},{8,4},{12,8},{16,12},{20,16},{24,20},{28,24},{0,28},{5,1},{9... | collective-permute-start | bytes 4718600 | tf_op jit(solution)/shard_map/ppermute | solution.py:94
  812.4 69.2 %collective-permute-start.3 = (bf16[2,768,512]{2,1,0:T(8,128)(2,1)}, bf16[2,768,512]{2,1,0:T(8,128)(2,1)}, u32[]{:S(2)}, u32[]{:S(2)}) collective-permute-start(bf16[2,768,512]{2,1,0:T(8,128)(2,1)} %collective-permute-done.2), channel_id=1, source_target_pairs={{0,4},{4,8},{8,12},{12,16},{16,20},{20,24},{24,28},{28,0},{1,5},{5... | collective-permute-start | bytes 4718600 | tf_op jit(solution)/shard_map/ppermute | solution.py:92
  846.5 50.4 %collective-permute-start.6 = (bf16[2,768,512]{2,1,0:T(8,128)(2,1)}, bf16[2,768,512]{2,1,0:T(8,128)(2,1)S(1)}, u32[]{:S(2)}, u32[]{:S(2)}) collective-permute-start(bf16[2,768,512]{2,1,0:T(8,128)(2,1)} %collective-permute-done.5), channel_id=1, source_target_pairs={{4,0},{8,4},{12,8},{16,12},{20,16},{24,20},{28,24},{0,28},{5,1},{9... | collective-permute-start | bytes 4718600 | tf_op jit(solution)/shard_map/ppermute | solution.py:94
  884.2 2.8 copy-start.4
  887.1 2.0 copy-start.2
Sparse Core Ops, SparseCore 0:
  150.7 207.6 reduce-scatter.1
  366.4 143.8 all-reduce.4
Sparse Core Ops, SparseCore 1:
  846.5 118.3 all-reduce.2
